TPU v7x, 32 devices: a whole 2x2x4 slice. The times are simulated.
32 devices in a mesh: groups: 2 (over x), ctx: 16 (over z, y, core).
Axes of the slice: x: 2, y: 2, z: 4, core: 2. Of those that a mesh axis runs over, the one named last changes fastest.
Arguments:
- queries: bfloat16 [4096, 8192], P(('groups', 'ctx')), parts along dimension 0, may hold values from -8 to 8
- new_keys: bfloat16 [4096, 1024], P(('groups', 'ctx')), parts along dimension 0, may hold values from -12 to 12
- new_values: bfloat16 [4096, 1024], P(('groups', 'ctx')), parts along dimension 0, may hold values from -6 to 6
- prefix_keys: bfloat16 [256, 1024], P(('groups', 'ctx')), parts along dimension 0, may hold values from -16 to 16
- prefix_values: bfloat16 [256, 1024], P(('groups', 'ctx')), parts along dimension 0, may hold values from -6 to 6
- pool_keys: bfloat16 [32, 2, 256, 1024], P(('groups', 'ctx')), parts along dimension 0, may hold values from -12 to 12
- pool_values: bfloat16 [32, 2, 256, 1024], P(('groups', 'ctx')), parts along dimension 0, may hold values from -6 to 6
- owners: int32 [4], P('groups'), parts along dimension 0, may hold values from 0 to 15
- lengths: int32 [32], P(('groups', 'ctx')), parts along dimension 0, may hold values from 1 to 128, as said below
Outputs:
- attended: bfloat16 [4096, 8192], P(('groups', 'ctx')), parts along dimension 0
There are 2 independent parts, one for each index of `groups`. A program takes and returns all parts, laid end to end along the dimension named above; each array names one. Nothing has to cross between parts.
Inputs may be any that keep to these rules, and one draw needn't show every extreme that they name: `lengths`: some device's prompt fills all 128 slots.
All inputs are finite; a program needn't handle non-finite values.
Results may differ from a plain program's by a relative error of at most 0.0035.
Values may be sent and summed in bfloat16 or wider, within the bound.
A program may use at most 128 MiB of HBM per device.

v0:
```python
import jax
import jax.numpy as jnp
from jax import lax
from jax.sharding import PartitionSpec as P

H = 64
KVH = 8
HD = 128
SB = 2
BLK = 256


def attend(carried, head_queries, key_rows, value_rows, visible):
    maxima, totals, accums = carried
    new_maxima = []
    new_totals = []
    new_accums = []
    score_scale = 1.0 / HD**0.5
    for kv_head in range(KVH):
        head_keys = key_rows[:, kv_head * HD : (kv_head + 1) * HD]
        head_values = value_rows[:, kv_head * HD : (kv_head + 1) * HD]
        scores = (
            lax.dot_general(
                head_queries[kv_head],
                head_keys,
                (((1,), (1,)), ((), ())),
                preferred_element_type=jnp.float32,
            )
            * score_scale
        )
        if visible is not None:
            scores = jnp.where(visible, scores, -1e30)
        new_max = jnp.maximum(maxima[kv_head], jnp.max(scores, axis=1))
        weights = jnp.exp(scores - new_max[:, None])
        if visible is not None:
            weights = jnp.where(visible, weights, 0.0)
        shrink = jnp.exp(maxima[kv_head] - new_max)
        new_totals.append(totals[kv_head] * shrink + jnp.sum(weights, axis=1))
        summed = jnp.dot(
            weights.astype(jnp.bfloat16), head_values, preferred_element_type=jnp.float32
        )
        new_accums.append(accums[kv_head] * shrink[:, None] + summed)
        new_maxima.append(new_max)
    return (jnp.stack(new_maxima), jnp.stack(new_totals), jnp.stack(new_accums))


def body(
    queries,
    new_keys,
    new_values,
    prefix_keys,
    prefix_values,
    pool_keys,
    pool_values,
    owners,
    lengths,
):
    group_size = H // KVH
    rows_here = queries.shape[0]
    head_queries = [
        queries[:, kv_head * group_size * HD : (kv_head + 1) * group_size * HD].reshape(
            rows_here * group_size, HD
        )
        for kv_head in range(KVH)
    ]
    carried = (
        jnp.full((KVH, rows_here * group_size), -1e30, jnp.float32),
        jnp.zeros((KVH, rows_here * group_size), jnp.float32),
        jnp.zeros((KVH, rows_here * group_size, HD), jnp.float32),
    )
    length = lengths[0]
    positions = jnp.arange(rows_here)
    own_visible = (positions[None, :] <= positions[:, None]) & (positions[None, :] < length)
    own_visible = jnp.repeat(own_visible, group_size, axis=0)
    carried = attend(carried, head_queries, new_keys, new_values, own_visible)
    pages_keys = pool_keys[0]
    pages_values = pool_values[0]
    my_rank = lax.axis_index("ctx")
    owned = (owners == my_rank)[:, None, None]
    mine_keys = jnp.where(owned, pages_keys.astype(jnp.float32), 0.0).reshape(SB * BLK, KVH * HD)
    mine_values = jnp.where(owned, pages_values.astype(jnp.float32), 0.0).reshape(
        SB * BLK, KVH * HD
    )
    part_keys, part_values = (
        lax.psum_scatter(mine_keys, "ctx", scatter_dimension=0, tiled=True),
        lax.psum_scatter(mine_values, "ctx", scatter_dimension=0, tiled=True),
    )
    shared_keys, shared_values = (
        lax.all_gather(part_keys.astype(jnp.bfloat16), "ctx", axis=0, tiled=True),
        lax.all_gather(part_values.astype(jnp.bfloat16), "ctx", axis=0, tiled=True),
    )
    carried = attend(carried, head_queries, shared_keys, shared_values, None)
    whole_keys, whole_values = (
        lax.all_gather(prefix_keys, "ctx", axis=0, tiled=True),
        lax.all_gather(prefix_values, "ctx", axis=0, tiled=True),
    )
    carried = attend(carried, head_queries, whole_keys, whole_values, None)
    maxima, totals, accums = carried
    pieces = [
        (accums[kv_head] / totals[kv_head][:, None]).reshape(rows_here, group_size * HD)
        for kv_head in range(KVH)
    ]
    joined = jnp.concatenate(pieces, axis=1)
    live = positions < length
    return jnp.where(live[:, None], joined, 0.0).astype(jnp.bfloat16)


def solution(mesh):
    placed = (
        P(("groups", "ctx"), None),
        P(("groups", "ctx"), None),
        P(("groups", "ctx"), None),
        P(("groups", "ctx"), None),
        P(("groups", "ctx"), None),
        P(("groups", "ctx"), None, None, None),
        P(("groups", "ctx"), None, None, None),
        P("groups"),
        P(("groups", "ctx")),
    )
    return jax.shard_map(
        body, mesh=mesh, in_specs=placed, out_specs=P(("groups", "ctx"), None), check_vma=False
    )
```

profile of v0, /device:TPU:0, one launch (start us, length us, event | category | flops | bytes accessed | tf_op | source)
XLA Modules:
  0.0 285.9 jit_solution(6476662964461193253)
XLA Ops:
  7.3 3.9 %convert_select_fusion = (f32[512,1024]{1,0:T(8,128)}, f32[512,1024]{1,0:T(8,128)}) fusion(bf16[1,2,256,1024]{3,2,1,0:T(8,128)(2,1)} %param.15, pred[512]{0:T(512)(128)(4,1)S(1)} %broadcast_in_dim.53, bf16[1,2,256,1024]{3,2,1,0:T(8,128)(2,1)} %param.14), kind=kLoop, calls=%fused_computation.1 | loop fusion | flops 2097152 | bytes 6291968 | tf_op jit(solution)/shard_map/jit(_where)/select_n | solution.py:81
  15.4 23.8 %all_gather.14 = bf16[128,1024]{1,0:T(8,128)(2,1)S(1)} all-gather(bf16[8,1024]{1,0:T(8,128)(2,1)S(1)} %copy-done.97), channel_id=1, replica_groups=mesh['groups'=2,'ctx'=16] {'ctx'}, dimensions={0}, use_global_device_ids=true | all-gather | bytes 278528 | tf_op jit(solution)/shard_map/all_gather | solution.py:94
  48.9 27.0 %reduce-scatter.3.cloned.1.call-done = f32[32,1024]{1,0:T(8,128)} async-done(((f32[512,1024]{1,0:T(8,128)}), f32[32,1024]{1,0:T(8,128)}) %reduce-scatter.3.cloned.1.call-update) | async-done | bytes 131088 | tf_op jit(solution)/shard_map/reduce_scatter | solution.py:85
  77.5 21.8 %all_gather.15 = bf16[128,1024]{1,0:T(8,128)(2,1)} all-gather(bf16[8,1024]{1,0:T(8,128)(2,1)} %param.13), channel_id=1, replica_groups=mesh['groups'=2,'ctx'=16] {'ctx'}, dimensions={0}, use_global_device_ids=true | all-gather | bytes 278528 | tf_op jit(solution)/shard_map/all_gather | solution.py:95
  112.9 27.5 %reduce-scatter.5.cloned.1.call-done = f32[32,1024]{1,0:T(8,128)} async-done(((f32[512,1024]{1,0:T(8,128)}), f32[32,1024]{1,0:T(8,128)}) %reduce-scatter.5.cloned.1.call-update) | async-done | bytes 131088 | tf_op jit(solution)/shard_map/reduce_scatter | solution.py:86
  142.0 37.4 %all-gather.3.cloned.1.call-done = bf16[512,1024]{1,0:T(8,128)(2,1)} async-done(((bf16[32,1024]{1,0:T(8,128)(2,1)}), bf16[512,1024]{1,0:T(8,128)(2,1)}) %all-gather.3.cloned.1.call-update) | async-done | bytes 1048592 | tf_op jit(solution)/shard_map/all_gather | solution.py:89
  184.0 2.1 fusion.120
  186.2 2.8 multiply_reduce_fusion.1
  194.4 1.8 multiply_reduce_fusion.3
  197.5 1.8 multiply_reduce_fusion.4
  200.6 1.8 multiply_reduce_fusion.5
  204.8 1.8 multiply_reduce_fusion.7
  215.6 2.0 fusion.41
  218.2 3.3 %fusion.54 = bf16[1024,128]{1,0:T(8,128)(2,1)} fusion(f32[1024,128]{1,0:T(8,128)} %fusion.132, f32[1024,128]{1,0:T(8,128)} %fusion.41, f32[512,1024]{1,0:T(8,128)} %copy-done.6, f32[1024]{0:T(1024)S(1)} %copy-done.84, f32[1024]{0:T(1024)S(1)} %get-tuple-element.43, f32[1024]{0:T(1024)S(1)} %get-tuple-element.44, ...), kind=kOutput, calls=%fused_computation.105 | convolution fusion | flops 136445952 | bytes 3551232 | tf_op jit(solution)/shard_map/dot_general | solution.py:39
  222.6 2.1 fusion.4
  227.0 2.5 fusion.53
  229.5 1.8 reshape.485
  231.3 2.1 fusion.6
  235.6 2.3 fusion.52
  237.9 1.8 reshape.487
  239.7 2.1 fusion.8
  244.1 2.3 fusion.51
  246.4 1.8 reshape.489
  248.2 2.1 fusion.10
  252.6 2.3 fusion.50
  254.9 1.8 reshape.491
  256.7 2.1 fusion.12
  261.1 2.3 fusion.49
  263.4 1.8 reshape.493
  270.0 2.0 fusion
  273.4 2.3 fusion.55
  277.6 1.8 select_convert_fusion
  (298 shorter events, 75.0 us)
Async XLA Ops:
  6.5 69.4 %reduce-scatter.3.cloned.1.call-start = ((), (), s32[]{:S(2)}) async-start(), calls=%async_computation.2 | async-start | bytes 2228224 | tf_op jit(solution)/shard_map/reduce_scatter | solution.py:85
  11.2 129.2 %reduce-scatter.5.cloned.1.call-start = ((), (), s32[]{:S(2)}) async-start(), calls=%async_computation.4 | async-start | bytes 2228224 | tf_op jit(solution)/shard_map/reduce_scatter | solution.py:86
  12.0 167.4 %all-gather.3.cloned.1.call-start = ((), (), s32[]{:S(2)}) async-start(), calls=%async_computation.3 | async-start | bytes 1114112 | tf_op jit(solution)/shard_map/all_gather | solution.py:89
  14.7 27.2 %copy-start.52 = (bf16[128,1024]{1,0:T(8,128)(2,1)S(1)}, bf16[128,1024]{1,0:T(8,128)(2,1)}, u32[]{:S(2)}) copy-start(bf16[128,1024]{1,0:T(8,128)(2,1)} %param.10) | copy-start | bytes 786436
  14.8 32.4 %copy-start.20 = (bf16[1024,128]{1,0:T(8,128)(2,1)}, bf16[1024,128]{1,0:T(8,128)(2,1)S(1)}, u32[]{:S(2)}) copy-start(bf16[1024,128]{1,0:T(8,128)(2,1)S(1)} %reshape.484) | copy-start | bytes 786436
  15.1 28.1 %copy-start.27 = (bf16[1024,128]{1,0:T(8,128)(2,1)}, bf16[1024,128]{1,0:T(8,128)(2,1)S(1)}, u32[]{:S(2)}) copy-start(bf16[1024,128]{1,0:T(8,128)(2,1)S(1)} %reshape.494) | copy-start | bytes 786436
  15.4 29.4 %copy-start.24 = (bf16[1024,128]{1,0:T(8,128)(2,1)}, bf16[1024,128]{1,0:T(8,128)(2,1)S(1)}, u32[]{:S(2)}) copy-start(bf16[1024,128]{1,0:T(8,128)(2,1)S(1)} %reshape.492) | copy-start | bytes 786436
  42.9 146.0 %copy-start.70 = (f32[1024]{0:T(1024)}, f32[1024]{0:T(1024)S(1)}, u32[]{:S(2)}) copy-start(f32[1024]{0:T(1024)S(1)} %get-tuple-element.95) | copy-start | bytes 12292
  43.2 137.8 %copy-start.68 = (f32[1024]{0:T(1024)}, f32[1024]{0:T(1024)S(1)}, u32[]{:S(2)}) copy-start(f32[1024]{0:T(1024)S(1)} %get-tuple-element.89) | copy-start | bytes 12292
  43.2 56.2 %copy-start.38 = (bf16[128,1024]{1,0:T(8,128)(2,1)S(1)}, bf16[128,1024]{1,0:T(8,128)(2,1)}, u32[]{:S(2)}) copy-start(bf16[128,1024]{1,0:T(8,128)(2,1)} %get-tuple-element.53) | copy-start | bytes 786436
  44.8 54.7 %copy-start.37 = (bf16[128,1024]{1,0:T(8,128)(2,1)S(1)}, bf16[128,1024]{1,0:T(8,128)(2,1)}, u32[]{:S(2)}) copy-start(bf16[128,1024]{1,0:T(8,128)(2,1)} %get-tuple-element.54) | copy-start | bytes 786436
  44.8 54.8 %copy-start.36 = (bf16[128,1024]{1,0:T(8,128)(2,1)S(1)}, bf16[128,1024]{1,0:T(8,128)(2,1)}, u32[]{:S(2)}) copy-start(bf16[128,1024]{1,0:T(8,128)(2,1)} %get-tuple-element.55) | copy-start | bytes 786436
  45.7 54.1 %copy-start.35 = (bf16[128,1024]{1,0:T(8,128)(2,1)S(1)}, bf16[128,1024]{1,0:T(8,128)(2,1)}, u32[]{:S(2)}) copy-start(bf16[128,1024]{1,0:T(8,128)(2,1)} %get-tuple-element.56) | copy-start | bytes 786436
  77.5 140.7 %all-gather.5.cloned.1.call-start = ((), (), s32[]{:S(2)}) async-start(), calls=%async_computation.5 | async-start | bytes 1114112 | tf_op jit(solution)/shard_map/all_gather | solution.py:90
  99.5 11.8 %copy-start.22 = (bf16[1024,128]{1,0:T(8,128)(2,1)}, bf16[1024,128]{1,0:T(8,128)(2,1)S(1)}, u32[]{:S(2)}) copy-start(bf16[1024,128]{1,0:T(8,128)(2,1)S(1)} %reshape.482) | copy-start | bytes 786436
  99.6 8.4 %copy-start.30 = (bf16[1024,128]{1,0:T(8,128)(2,1)}, bf16[1024,128]{1,0:T(8,128)(2,1)S(1)}, u32[]{:S(2)}) copy-start(bf16[1024,128]{1,0:T(8,128)(2,1)S(1)} %reshape.490) | copy-start | bytes 786436
  99.7 8.3 %copy-start.28 = (bf16[1024,128]{1,0:T(8,128)(2,1)}, bf16[1024,128]{1,0:T(8,128)(2,1)S(1)}, u32[]{:S(2)}) copy-start(bf16[1024,128]{1,0:T(8,128)(2,1)S(1)} %reshape.488) | copy-start | bytes 786436
  99.9 8.1 %copy-start.25 = (bf16[1024,128]{1,0:T(8,128)(2,1)}, bf16[1024,128]{1,0:T(8,128)(2,1)S(1)}, u32[]{:S(2)}) copy-start(bf16[1024,128]{1,0:T(8,128)(2,1)S(1)} %reshape.486) | copy-start | bytes 786436
  179.4 6.8 %copy-start.33 = (bf16[512,1024]{1,0:T(8,128)(2,1)S(1)}, bf16[512,1024]{1,0:T(8,128)(2,1)}, u32[]{:S(2)}) copy-start(bf16[512,1024]{1,0:T(8,128)(2,1)} %all-gather.3.cloned.1.call-done) | copy-start | bytes 3145732
  180.9 8.6 %copy-start.19 = (f32[1024,128]{0,1:T(8,128)S(1)}, f32[1024,128]{0,1:T(8,128)}, u32[]{:S(2)}) copy-start(f32[1024,128]{0,1:T(8,128)} %get-tuple-element.92) | copy-start | bytes 1572868
  182.3 24.9 %copy-start.56 = (f32[1024]{0:T(1024)}, f32[1024]{0:T(1024)S(1)}, u32[]{:S(2)}) copy-start(f32[1024]{0:T(1024)S(1)} %get-tuple-element.62) | copy-start | bytes 12292
  184.0 6.2 %copy-start.34 = (bf16[128,1024]{1,0:T(8,128)(2,1)S(1)}, bf16[128,1024]{1,0:T(8,128)(2,1)}, u32[]{:S(2)}) copy-start(bf16[128,1024]{1,0:T(8,128)(2,1)} %all_gather.15) | copy-start | bytes 786436
  186.2 5.1 %copy-start.31 = (bf16[1024,128]{1,0:T(8,128)(2,1)S(1)}, bf16[1024,128]{1,0:T(8,128)(2,1)}, u32[]{:S(2)}) copy-start(bf16[1024,128]{1,0:T(8,128)(2,1)} %copy-done.30) | copy-start | bytes 786436
  189.6 17.6 %copy-start.58 = (f32[1024]{0:T(1024)}, f32[1024]{0:T(1024)S(1)}, u32[]{:S(2)}) copy-start(f32[1024]{0:T(1024)S(1)} %get-tuple-element.64) | copy-start | bytes 12292
  193.7 13.5 %copy-start.62 = (f32[1024]{0:T(1024)}, f32[1024]{0:T(1024)S(1)}, u32[]{:S(2)}) copy-start(f32[1024]{0:T(1024)S(1)} %get-tuple-element.66) | copy-start | bytes 12292
  196.8 10.4 %copy-start.63 = (f32[1024]{0:T(1024)}, f32[1024]{0:T(1024)S(1)}, u32[]{:S(2)}) copy-start(f32[1024]{0:T(1024)S(1)} %get-tuple-element.68) | copy-start | bytes 12292
  196.8 13.5 %copy-start.53 = (f32[1024]{0:T(1024)}, f32[1024]{0:T(1024)S(1)}, u32[]{:S(2)}) copy-start(f32[1024]{0:T(1024)S(1)} %get-tuple-element.31) | copy-start | bytes 12292
  199.9 7.3 %copy-start.64 = (f32[1024]{0:T(1024)}, f32[1024]{0:T(1024)S(1)}, u32[]{:S(2)}) copy-start(f32[1024]{0:T(1024)S(1)} %get-tuple-element.70) | copy-start | bytes 12292
  199.9 11.4 %copy-start.54 = (f32[1024]{0:T(1024)}, f32[1024]{0:T(1024)S(1)}, u32[]{:S(2)}) copy-start(f32[1024]{0:T(1024)S(1)} %get-tuple-element.36) | copy-start | bytes 12292
  203.0 9.4 %copy-start.55 = (f32[1024]{0:T(1024)}, f32[1024]{0:T(1024)S(1)}, u32[]{:S(2)}) copy-start(f32[1024]{0:T(1024)S(1)} %get-tuple-element.41) | copy-start | bytes 12292
  204.2 4.9 %copy-start.83 = (f32[1024]{0:T(1024)}, f32[1024]{0:T(1024)S(1)}, u32[]{:S(2)}) copy-start(f32[1024]{0:T(1024)S(1)} %get-tuple-element.47) | copy-start | bytes 12292
  212.4 5.9 %copy-start.84 = (f32[1024]{0:T(1024)S(1)}, f32[1024]{0:T(1024)}, u32[]{:S(2)}) copy-start(f32[1024]{0:T(1024)} %copy-done.83) | copy-start | bytes 12292
  (72 other events, 221.2 us)
Sparse Core Ops, SparseCore 0:
  11.4 64.5 reduce-scatter.2
  79.7 60.6 reduce-scatter.4
  142.6 36.7 all-gather.2
  181.4 36.7 all-gather.4
where the time goes:
time: 287 us; the launch traced here: 286 us
  waiting for transfers between devices  93.3 us (33%)
  matrix products  76.8 us (27%)
  blocking collectives  45.6 us (16%)
  other arithmetic  38.8 us (14%)
  local copies, waits for them, and re-layouts  16.5 us (6%)
  between operations  14.9 us (5%)
    dot_general x24, matrix products, attend(): jnp.dot(weights.astype(jnp.bfloat16), head_values, preferred_element_type...  40.5 us
    all_gather x1, waiting for transfers between devices, body(): lax.all_gather(part_keys.astype(jnp.bfloat16), 'ctx', axis=0, tiled=True)  37.4 us
    dot_general x24, matrix products, attend(): lax.dot_general(head_queries[kv_head], head_keys, (((1,), (1,)), ((), ())...  36.3 us
    reduce_scatter x1, waiting for transfers between devices, body(): lax.psum_scatter(mine_values, 'ctx', scatter_dimension=0, tiled=True)  27.5 us
    reduce_scatter x1, waiting for transfers between devices, body(): lax.psum_scatter(mine_keys, 'ctx', scatter_dimension=0, tiled=True)  27 us
    all_gather x1, blocking collectives, body(): lax.all_gather(prefix_keys, 'ctx', axis=0, tiled=True)  23.8 us
    all_gather x1, blocking collectives, body(): lax.all_gather(prefix_values, 'ctx', axis=0, tiled=True)  21.8 us
    reduce_sum x16, other arithmetic, attend(): new_totals.append(totals[kv_head] * shrink + jnp.sum(weights, axis=1))  20.7 us
  transfers between devices with their start and end apart: 4, of which 4 were waited for; matrix products, arithmetic and copies ran while one was open for 23% of the time, Pallas kernels for 0%

commit v1 on v0

v1 whole, which is shorter than its diff:
```python
import functools

import jax
import jax.numpy as jnp
from jax import lax
from jax.experimental import pallas as pl
from jax.experimental.pallas import tpu as pltpu
from jax.sharding import PartitionSpec as P

HD = 128
SIB_STEPS = 1
HOP_STEPS = 2
HEADS_AT_ONCE = 4


def grid_of(ring):
    chips = ring // 2
    short = 1
    while (short * 2) ** 2 <= chips and chips % (short * 2) == 0:
        short *= 2
    return chips // short, short


def kernel(
    ring, heads, kv_heads,
    q_ref, nk_ref, nv_ref, pk_ref, pv_ref, poolk_ref, poolv_ref, owners_ref, lengths_ref,
    out_ref,
    x, sib_s, sib_r, yu_s, yu_r, yd_s, yd_r, xy, zu_s, zu_r, zd_s, zd_r, kvf, bias,
    send_sems, recv_sems,
):
    long, short = grid_of(ring)
    me = lax.axis_index("ctx")
    core = lax.rem(me, 2)
    chip = lax.div(me, 2)
    py = lax.rem(chip, short)
    pz = lax.div(chip, short)
    sibling = me + 1 - 2 * core
    blocks, blk = poolk_ref.shape[1], poolk_ref.shape[2]
    chunks = kv_heads * blocks
    own_rows = pk_ref.shape[0]
    pre = own_rows * ring // blocks
    rows = q_ref.shape[0]
    group = heads // kv_heads

    barrier = pltpu.get_barrier_semaphore()

    def greet(target):
        pl.semaphore_signal(barrier, inc=1, device_id={"ctx": target})

    greet(sibling)
    for pos, size, step in ((py, short, 2), (pz, long, 2 * short)):
        @pl.when(pos > 0)
        def _():
            greet(me - step)

        @pl.when(pos < size - 1)
        def _():
            greet(me + step)

    peers = 1
    for pos, size in ((py, short), (pz, long)):
        peers = peers + jnp.where(pos > 0, 1, 0) + jnp.where(pos < size - 1, 1, 0)
    pl.semaphore_wait(barrier, peers)

    def remote(kind, i, src, dst, target):
        return pltpu.make_async_remote_copy(
            src_ref=src, dst_ref=dst, send_sem=send_sems.at[kind, i], recv_sem=recv_sems.at[kind, i],
            device_id={"ctx": target}, device_id_type=pl.DeviceIdType.MESH,
        )

    length = lengths_ref[0]
    tok = lax.broadcasted_iota(jnp.int32, (rows, rows), 0)
    key = lax.broadcasted_iota(jnp.int32, (rows, rows), 1)
    bias[...] = jnp.where((key <= tok) & (key < length), 0.0, -1e30)

    def cols(g):
        return pl.ds(pl.multiple_of(g * HD, HD), HD)

    def build(i):
        g, b = lax.div(i, blocks), lax.rem(i, blocks)
        mine = jnp.where(owners_ref[b] == me, 1.0, 0.0).astype(jnp.float32)
        row = lax.broadcasted_iota(jnp.int32, (pre, HD), 0) + b * pre
        in_mine = (row >= me * own_rows) & (row < (me + 1) * own_rows)
        parts = []
        for pool, pre_ref in ((poolk_ref, pk_ref), (poolv_ref, pv_ref)):
            page = pool[0, b, :, cols(g)]
            page = page * jnp.full(page.shape, mine, jnp.float32).astype(jnp.bfloat16)
            mine_pre = pre_ref[:, cols(g)].astype(jnp.float32)
            tiled = jnp.concatenate([mine_pre] * (pre // own_rows), axis=0)
            parts.append((page, jnp.where(in_mine, tiled, 0.0).astype(jnp.bfloat16)))
        is_k = core == 0

        @pl.when(is_k)
        def _():
            x[i, :blk], x[i, blk:] = parts[0]
            sib_s[i, :blk], sib_s[i, blk:] = parts[1]

        @pl.when(jnp.logical_not(is_k))
        def _():
            x[i, :blk], x[i, blk:] = parts[1]
            sib_s[i, :blk], sib_s[i, blk:] = parts[0]

    def valid(i):
        return (i >= 0) & (i < chunks)

    def scan(t, kind, pos, size, step, base, src, up_s, up_r, dn_s, dn_r, write):
        up = t - base - pos * HOP_STEPS

        @pl.when(valid(up))
        def _():
            @pl.when(pos > 0)
            def _():
                remote(kind, up, up_s.at[up], up_r.at[up], me - step).wait_recv()

            @pl.when((pos > 0) & (pos < size - 1))
            def _():
                up_s[up] = src[up] + up_r[up]

            @pl.when((pos == 0) & (pos < size - 1))
            def _():
                up_s[up] = src[up]

            @pl.when(pos < size - 1)
            def _():
                remote(kind, up, up_s.at[up], up_r.at[up], me + step).start()

        dn = t - base - (size - 1 - pos) * HOP_STEPS

        @pl.when(valid(dn))
        def _():
            @pl.when(pos < size - 1)
            def _():
                remote(kind + 1, dn, dn_s.at[dn], dn_r.at[dn], me + step).wait_recv()

            @pl.when((pos > 0) & (pos < size - 1))
            def _():
                dn_s[dn] = src[dn] + dn_r[dn]

            @pl.when((pos > 0) & (pos == size - 1))
            def _():
                dn_s[dn] = src[dn]

            @pl.when(pos > 0)
            def _():
                remote(kind + 1, dn, dn_s.at[dn], dn_r.at[dn], me - step).start()

        end = t - base - (size - 1) * HOP_STEPS

        @pl.when(valid(end))
        def _():
            @pl.when((pos > 0) & (pos < size - 1))
            def _():
                write(end, src[end] + up_r[end] + dn_r[end])

            @pl.when((pos > 0) & (pos == size - 1))
            def _():
                write(end, src[end] + up_r[end])

            @pl.when((pos == 0) & (pos < size - 1))
            def _():
                write(end, src[end] + dn_r[end])

            if size == 1:
                write(end, src[end])

        return base + (size - 1) * HOP_STEPS

    live = lax.broadcasted_iota(jnp.int32, (rows, HD), 0) < length
    batches = group // HEADS_AT_ONCE
    score_scale = 1.0 / HD**0.5
    all_rows = blocks * (blk + pre)

    def attend(m):
        g, part = lax.div(m, batches), lax.rem(m, batches)
        first = g * group + part * HEADS_AT_ONCE
        q = jnp.concatenate([q_ref[:, cols(first + j)] for j in range(HEADS_AT_ONCE)], axis=0)
        keys = kvf[0, pl.ds(g * blocks, blocks)].reshape(all_rows, HD)
        values = kvf[1, pl.ds(g * blocks, blocks)].reshape(all_rows, HD)
        dims = (((1,), (1,)), ((), ()))
        s_far = lax.dot_general(q, keys, dims, preferred_element_type=jnp.float32) * score_scale
        s_own = lax.dot_general(q, nk_ref[:, cols(g)], dims, preferred_element_type=jnp.float32)
        s_own = s_own * score_scale + jnp.concatenate([bias[...]] * HEADS_AT_ONCE, axis=0)
        top = jnp.maximum(jnp.max(s_far, axis=1, keepdims=True), jnp.max(s_own, axis=1, keepdims=True))
        w_far = jnp.exp(s_far - top).astype(jnp.bfloat16)
        w_own = jnp.exp(s_own - top).astype(jnp.bfloat16)
        v_far = jnp.concatenate([values, jnp.ones_like(values)], axis=1)
        own = nv_ref[:, cols(g)]
        v_own = jnp.concatenate([own, jnp.ones_like(own)], axis=1)
        summed = jnp.dot(w_far, v_far, preferred_element_type=jnp.float32)
        summed += jnp.dot(w_own, v_own, preferred_element_type=jnp.float32)
        result = summed[:, :HD] / summed[:, HD:]
        for j in range(HEADS_AT_ONCE):
            piece = jnp.where(live, result[j * rows : (j + 1) * rows], 0.0)
            out_ref[:, cols(first + j)] = piece.astype(out_ref.dtype)

    def finish(i, value):
        kvf[core, i] = value
        remote(5, i, kvf.at[core, i], kvf.at[core, i], sibling).start()

    y_base = SIB_STEPS
    z_base = y_base + (short - 1) * HOP_STEPS
    f_base = z_base + (long - 1) * HOP_STEPS
    c_base = f_base + SIB_STEPS
    attends = kv_heads * batches
    steps = c_base + max(chunks + 1, attends + blocks)

    def one_step(t, carry):
        @pl.when(t < chunks)
        def _():
            build(t)
            remote(0, t, sib_s.at[t], sib_r.at[t], sibling).start()

        i = t - y_base

        @pl.when(valid(i))
        def _():
            remote(0, i, sib_s.at[i], sib_r.at[i], sibling).wait_recv()
            x[i] = x[i] + sib_r[i]

        def write_xy(i, value):
            xy[i] = value

        scan(t, 1, py, short, 2, y_base, x, yu_s, yu_r, yd_s, yd_r, write_xy)
        scan(t, 3, pz, long, 2 * short, z_base, xy, zu_s, zu_r, zd_s, zd_r, finish)
        i_c = t - c_base

        @pl.when(valid(i_c))
        def _():
            remote(5, i_c, kvf.at[core, i_c], kvf.at[1 - core, i_c], sibling).wait_recv()

        m = t - c_base - (blocks - 1)

        @pl.when((m >= 0) & (m < attends))
        def _():
            attend(m)

        return carry

    lax.fori_loop(0, steps, one_step, 0)

    def drain(i, carry):
        remote(0, i, sib_s.at[i], sib_r.at[i], sibling).wait_send()
        remote(5, i, kvf.at[core, i], kvf.at[core, i], sibling).wait_send()
        for kind, pos, size, step, up_s, up_r, dn_s, dn_r in (
            (1, py, short, 2, yu_s, yu_r, yd_s, yd_r),
            (3, pz, long, 2 * short, zu_s, zu_r, zd_s, zd_r),
        ):
            @pl.when(pos < size - 1)
            def _():
                remote(kind, i, up_s.at[i], up_r.at[i], me + step).wait_send()

            @pl.when(pos > 0)
            def _():
                remote(kind + 1, i, dn_s.at[i], dn_r.at[i], me - step).wait_send()

        return carry

    lax.fori_loop(0, chunks, drain, 0)


def solution(mesh):
    ring = mesh.shape["ctx"]

    def body(queries, new_keys, new_values, prefix_keys, prefix_values, pool_keys, pool_values, owners, lengths):
        heads = queries.shape[1] // HD
        kv_heads = new_keys.shape[1] // HD
        blocks, blk = pool_keys.shape[1], pool_keys.shape[2]
        chunks = kv_heads * blocks
        c_rows = blk + prefix_keys.shape[0] * ring // blocks
        chunk_buf = pltpu.VMEM((chunks, c_rows, HD), jnp.bfloat16)
        vm = pl.BlockSpec(memory_space=pltpu.VMEM)
        sm = pl.BlockSpec(memory_space=pltpu.SMEM)
        return pl.pallas_call(
            functools.partial(kernel, ring, heads, kv_heads),
            out_shape=jax.ShapeDtypeStruct(queries.shape, jnp.bfloat16),
            in_specs=[vm] * 7 + [sm] * 2,
            out_specs=vm,
            scratch_shapes=[chunk_buf] * 12
            + [
                pltpu.VMEM((2, chunks, c_rows, HD), jnp.bfloat16),
                pltpu.VMEM((queries.shape[0], queries.shape[0]), jnp.float32),
                pltpu.SemaphoreType.DMA((6, chunks)),
                pltpu.SemaphoreType.DMA((6, chunks)),
            ],
            compiler_params=pltpu.CompilerParams(
                collective_id=0, has_side_effects=True, vmem_limit_bytes=67043328
            ),
        )(queries, new_keys, new_values, prefix_keys, prefix_values, pool_keys, pool_values, owners, lengths)

    two = P(("groups", "ctx"), None)
    four = P(("groups", "ctx"), None, None, None)
    return jax.shard_map(
        body, mesh=mesh, in_specs=(two,) * 5 + (four,) * 2 + (P("groups"), P(("groups", "ctx"))),
        out_specs=two, check_vma=False,
    )
```

time: 287 us -> 62.9 us (0.22)
  waiting for transfers between devices: 93.3 us -> 0 us
  matrix products: 76.8 us -> 0 us
  Pallas kernels: 0 us -> 58.9 us
  blocking collectives: 45.6 us -> 0 us
  other arithmetic: 38.8 us -> 0 us
  between operations: 14.9 us -> 0.66 us
  local copies, waits for them, and re-layouts: 16.5 us -> 3.1 us
    dot_general x48 -> x0, matrix products: 76.8 us -> none  [the longest x24 40.5 us: attend(): jnp.dot(weights.astype(jnp.bfloat16), head_values, preferred_element_type...]
    pallas_call x0 -> x1, Pallas kernels: none -> 58.9 us  [body(): pl.pallas_call(functools.partial(kernel, ring, heads, kv_heads), out_shap...]
    reduce_scatter x2 -> x0, waiting for transfers between devices: 54.5 us -> none  [the longest x1 27.5 us: body(): lax.psum_scatter(mine_values, 'ctx', scatter_dimension=0, tiled=True)]
    all_gather x2 -> x0, blocking collectives: 45.6 us -> none  [the longest x1 23.8 us: body(): lax.all_gather(prefix_keys, 'ctx', axis=0, tiled=True)]
    all_gather x2 -> x0, waiting for transfers between devices: 38 us -> none  [the longest x1 37.4 us: body(): lax.all_gather(part_keys.astype(jnp.bfloat16), 'ctx', axis=0, tiled=True)]
    reduce_sum x16 -> x0, other arithmetic: 20.7 us -> none  [attend(): new_totals.append(totals[kv_head] * shrink + jnp.sum(weights, axis=1))]
    reshape x18 -> x0, local copies, waits for them, and re-layouts: 13.1 us -> none  [the longest x8 11.9 us: body(): (accums[kv_head] / totals[kv_head][:, None]).reshape(rows_here, group_siz...]
    max x8 -> x0, other arithmetic: 4.97 us -> none  [attend(): new_max = jnp.maximum(maxima[kv_head], jnp.max(scores, axis=1))]
  transfers between devices with their start and end apart: 4 -> 0, of which waited for: 4 -> 0; matrix products, arithmetic and copies ran while one was open for 23% -> 0% of each run, Pallas kernels for 0% -> 0%
where the time goes in v1:
time: 62.9 us; the launch traced here: 62.7 us
  Pallas kernels  58.9 us (94%)
  local copies, waits for them, and re-layouts  3.1 us (5%)
  between operations  0.66 us (1%)
    pallas_call x1, Pallas kernels, body(): pl.pallas_call(functools.partial(kernel, ring, heads, kv_heads), out_shap...  58.9 us
    unnamed x1, local copies, waits for them, and re-layouts  3.1 us

profile of v1, /device:TPU:0, one launch (start us, length us, event | category | flops | bytes accessed | tf_op | source)
XLA Modules:
  0.0 62.7 jit_solution(17654695795105095464)
XLA Ops:
  0.7 58.9 %shard_map.91 = bf16[128,8192]{1,0:T(8,128)(2,1)} custom-call(bf16[128,8192]{1,0:T(8,128)(2,1)} %q_ref.1, bf16[128,1024]{1,0:T(8,128)(2,1)} %nk_ref.1, bf16[128,1024]{1,0:T(8,128)(2,1)} %nv_ref.1, bf16[8,1024]{1,0:T(8,128)(2,1)} %pk_ref.1, bf16[8,1024]{1,0:T(8,128)(2,1)} %pv_ref.1, bf16[1,2,256,1024]{3,2,1,0:T(8,128)(2,1)} %poolk_ref.1, ...), custom_call_target="tpu_custom_call" | custom-call | tf_op jit(solution)/shard_map/pallas_call | solution.py:273
  59.6 3.1 %copy.12 = bf16[128,8192]{1,0:T(8,128)(2,1)} copy(bf16[128,8192]{1,0:T(8,128)(2,1)} %shard_map.91) | data formatting | bytes 4194304

commit v2 on v1

v2 whole, which is shorter than its diff:
```python
import functools

import jax
import jax.numpy as jnp
from jax import lax
from jax.experimental import pallas as pl
from jax.experimental.pallas import tpu as pltpu
from jax.sharding import PartitionSpec as P

HD = 128
SIB_STEPS = 1
HOP_STEPS = 3
CUTS = 1
HEADS_AT_ONCE = 4


def grid_of(ring):
    chips = ring // 2
    short = 1
    while (short * 2) ** 2 <= chips and chips % (short * 2) == 0:
        short *= 2
    return chips // short, short


def kernel(
    ring, heads, kv_heads,
    q_hbm, nk_ref, nv_ref, pk_ref, pv_ref, poolk_ref, poolv_ref, owners_ref, lengths_ref,
    out_hbm,
    x, sib_s, sib_r, in_up, in_dn, up_s, up_r, dn_s, dn_r, kvf, bias, q_ref, out_ref,
    send_sems, recv_sems, q_sem, out_sems,
):
    long, short = grid_of(ring)
    me = lax.axis_index("ctx")
    core = lax.rem(me, 2)
    chip = lax.div(me, 2)
    py = lax.rem(chip, short)
    pz = lax.div(chip, short)
    sibling = me + 1 - 2 * core
    pieces = poolk_ref.shape[1] * CUTS
    blk = poolk_ref.shape[2] // CUTS
    chunks = kv_heads * pieces
    own_rows = pk_ref.shape[0]
    pre = own_rows * ring // pieces
    rows = q_hbm.shape[0]
    group = heads // kv_heads

    q_copy = pltpu.make_async_copy(q_hbm, q_ref, q_sem)
    q_copy.start()
    barrier = pltpu.get_barrier_semaphore()

    def greet(target):
        pl.semaphore_signal(barrier, inc=1, device_id={"ctx": target})

    greet(sibling)
    for pos, size, step in ((py, short, 2), (pz, long, 2 * short)):
        @pl.when(pos > 0)
        def _():
            greet(me - step)

        @pl.when(pos < size - 1)
        def _():
            greet(me + step)

    peers = 1
    for pos, size in ((py, short), (pz, long)):
        peers = peers + jnp.where(pos > 0, 1, 0) + jnp.where(pos < size - 1, 1, 0)
    pl.semaphore_wait(barrier, peers)

    def remote(kind, i, src, dst, target):
        return pltpu.make_async_remote_copy(
            src_ref=src, dst_ref=dst, send_sem=send_sems.at[kind, i], recv_sem=recv_sems.at[kind, i],
            device_id={"ctx": target}, device_id_type=pl.DeviceIdType.MESH,
        )

    length = lengths_ref[0]
    tok = lax.broadcasted_iota(jnp.int32, (rows, rows), 0)
    key = lax.broadcasted_iota(jnp.int32, (rows, rows), 1)
    bias[...] = jnp.where((key <= tok) & (key < length), 0.0, -1e30)

    def cols(g):
        return pl.ds(pl.multiple_of(g * HD, HD), HD)

    def build(i):
        g, b = lax.div(i, pieces), lax.rem(i, pieces)
        page_of = lax.div(b, CUTS)
        start = pl.multiple_of(lax.rem(b, CUTS) * blk, blk)
        mine = jnp.where(owners_ref[page_of] == me, 1.0, 0.0).astype(jnp.float32)
        row = lax.broadcasted_iota(jnp.int32, (pre, HD), 0) + b * pre
        in_mine = (row >= me * own_rows) & (row < (me + 1) * own_rows)
        parts = []
        for pool, pre_ref in ((poolk_ref, pk_ref), (poolv_ref, pv_ref)):
            page = pool[0, page_of, pl.ds(start, blk), cols(g)]
            page = page * jnp.full(page.shape, mine, jnp.float32).astype(jnp.bfloat16)
            mine_pre = pre_ref[:, cols(g)].astype(jnp.float32)
            tiled = jnp.concatenate([mine_pre] * (pre // own_rows), axis=0)
            parts.append((page, jnp.where(in_mine, tiled, 0.0).astype(jnp.bfloat16)))
        is_k = core == 0

        @pl.when(is_k)
        def _():
            x[i, :blk], x[i, blk:] = parts[0]
            sib_s[i, :blk], sib_s[i, blk:] = parts[1]

        @pl.when(jnp.logical_not(is_k))
        def _():
            x[i, :blk], x[i, blk:] = parts[1]
            sib_s[i, :blk], sib_s[i, blk:] = parts[0]

    def valid(i):
        return (i >= 0) & (i < chunks)

    first_is_y = core == 0

    def pick(if_y, if_z):
        return jnp.where(first_is_y, if_y, if_z)

    p1, l1, s1 = pick(py, pz), pick(short, long), pick(2, 2 * short)
    p2, l2, s2 = pick(pz, py), pick(long, short), pick(2 * short, 2)
    depth = lax.div(l1, 2)
    even = 1 - lax.rem(l1, 2)
    r_base = SIB_STEPS
    s_base = r_base + depth * HOP_STEPS
    b_base = s_base + (l2 - 1) * HOP_STEPS

    def root(i):
        return depth - lax.rem(i, 2) * even

    def in_up_copy(i):
        return remote(1, i, x.at[i], in_up.at[i], me + s1)

    def in_dn_copy(i):
        return remote(2, i, x.at[i], in_dn.at[i], me - s1)

    def up_copy(i):
        return remote(3, i, up_s.at[i], up_r.at[i], me + s2)

    def dn_copy(i):
        return remote(4, i, dn_s.at[i], dn_r.at[i], me - s2)

    def share_copy(i):
        return remote(5, i, kvf.at[core, i], kvf.at[core, i], sibling)

    def out_up_copy(i):
        return remote(6, i, kvf.at[core, i], kvf.at[core, i], me + s1)

    def out_dn_copy(i):
        return remote(7, i, kvf.at[core, i], kvf.at[core, i], me - s1)

    def gather_in(t):
        iu = t - r_base - p1 * HOP_STEPS

        @pl.when(valid(iu))
        def _():
            @pl.when(p1 < root(iu))
            def _():
                @pl.when(p1 > 0)
                def _():
                    in_up_copy(iu).wait_recv()
                    x[iu] = x[iu] + in_up[iu]

                in_up_copy(iu).start()

        dn = t - r_base - (l1 - 1 - p1) * HOP_STEPS

        @pl.when(valid(dn))
        def _():
            @pl.when(p1 > root(dn))
            def _():
                @pl.when(p1 < l1 - 1)
                def _():
                    in_dn_copy(dn).wait_recv()
                    x[dn] = x[dn] + in_dn[dn]

                in_dn_copy(dn).start()

        ir = t - s_base

        @pl.when(valid(ir))
        def _():
            @pl.when(p1 == root(ir))
            def _():
                @pl.when(p1 > 0)
                def _():
                    in_up_copy(ir).wait_recv()
                    x[ir] = x[ir] + in_up[ir]

                @pl.when(p1 < l1 - 1)
                def _():
                    in_dn_copy(ir).wait_recv()
                    x[ir] = x[ir] + in_dn[ir]

    def across(t):
        up = t - s_base - p2 * HOP_STEPS

        @pl.when(valid(up))
        def _():
            @pl.when(p1 == root(up))
            def _():
                @pl.when(p2 > 0)
                def _():
                    up_copy(up).wait_recv()

                @pl.when(p2 < l2 - 1)
                def _():
                    @pl.when(p2 > 0)
                    def _():
                        up_s[up] = x[up] + up_r[up]

                    @pl.when(p2 == 0)
                    def _():
                        up_s[up] = x[up]

                    up_copy(up).start()

        dn = t - s_base - (l2 - 1 - p2) * HOP_STEPS

        @pl.when(valid(dn))
        def _():
            @pl.when(p1 == root(dn))
            def _():
                @pl.when(p2 < l2 - 1)
                def _():
                    dn_copy(dn).wait_recv()

                @pl.when(p2 > 0)
                def _():
                    @pl.when(p2 < l2 - 1)
                    def _():
                        dn_s[dn] = x[dn] + dn_r[dn]

                    @pl.when(p2 == l2 - 1)
                    def _():
                        dn_s[dn] = x[dn]

                    dn_copy(dn).start()

    def spread(t):
        end = t - b_base

        @pl.when(valid(end))
        def _():
            @pl.when(p1 == root(end))
            def _():
                @pl.when((p2 > 0) & (p2 < l2 - 1))
                def _():
                    kvf[core, end] = x[end] + up_r[end] + dn_r[end]

                @pl.when((p2 > 0) & (p2 == l2 - 1))
                def _():
                    kvf[core, end] = x[end] + up_r[end]

                @pl.when((p2 == 0) & (p2 < l2 - 1))
                def _():
                    kvf[core, end] = x[end] + dn_r[end]

                @pl.when(l2 == 1)
                def _():
                    kvf[core, end] = x[end]

                @pl.when(p1 < l1 - 1)
                def _():
                    out_up_copy(end).start()

                @pl.when(p1 > 0)
                def _():
                    out_dn_copy(end).start()

                share_copy(end).start()

        for back in (0, 1):
            above = p1 - (depth - back)
            i = t - b_base - jnp.where(above > 0, above, -above) * HOP_STEPS

            @pl.when(valid(i) & (above != 0))
            def _():
                @pl.when(root(i) == depth - back)
                def _():
                    @pl.when(above > 0)
                    def _():
                        out_up_copy(i).wait_recv()

                        @pl.when(p1 < l1 - 1)
                        def _():
                            out_up_copy(i).start()

                    @pl.when(above < 0)
                    def _():
                        out_dn_copy(i).wait_recv()

                        @pl.when(p1 > 0)
                        def _():
                            out_dn_copy(i).start()

                    share_copy(i).start()

    live = lax.broadcasted_iota(jnp.int32, (rows, HD), 0) < length
    batches = group // HEADS_AT_ONCE
    score_scale = 1.4426950408889634 / HD**0.5
    wide = HEADS_AT_ONCE * HD

    def result_copy(m):
        columns = pl.ds(pl.multiple_of(m * wide, wide), wide)
        return pltpu.make_async_copy(out_ref.at[:, columns], out_hbm.at[:, columns], out_sems.at[m])

    all_rows = pieces * (blk + pre)

    def attend(m):
        g, part = lax.div(m, batches), lax.rem(m, batches)
        first = g * group + part * HEADS_AT_ONCE
        q = jnp.concatenate([q_ref[:, cols(first + j)] for j in range(HEADS_AT_ONCE)], axis=0)
        keys = kvf[0, pl.ds(g * pieces, pieces)].reshape(all_rows, HD)
        values = kvf[1, pl.ds(g * pieces, pieces)].reshape(all_rows, HD)
        dims = (((1,), (1,)), ((), ()))
        s_far = lax.dot_general(q, keys, dims, preferred_element_type=jnp.float32)
        s_own = lax.dot_general(q, nk_ref[:, cols(g)], dims, preferred_element_type=jnp.float32)
        s_own = s_own + jnp.concatenate([bias[...]] * HEADS_AT_ONCE, axis=0)
        top = jnp.maximum(jnp.max(s_far, axis=1, keepdims=True), jnp.max(s_own, axis=1, keepdims=True))
        w_far = jnp.exp2((s_far - top) * score_scale).astype(jnp.bfloat16)
        w_own = jnp.exp2((s_own - top) * score_scale).astype(jnp.bfloat16)
        v_far = jnp.concatenate([values, jnp.ones_like(values)], axis=1)
        own = nv_ref[:, cols(g)]
        v_own = jnp.concatenate([own, jnp.ones_like(own)], axis=1)
        summed = jnp.dot(w_far, v_far, preferred_element_type=jnp.float32)
        summed += jnp.dot(w_own, v_own, preferred_element_type=jnp.float32)
        result = summed[:, :HD] / summed[:, HD:]
        for j in range(HEADS_AT_ONCE):
            piece = jnp.where(live, result[j * rows : (j + 1) * rows], 0.0)
            out_ref[:, cols(first + j)] = piece.astype(out_ref.dtype)

    hops = max(2 * (short // 2) + long - 1, 2 * (long // 2) + short - 1)
    c_base = SIB_STEPS + hops * HOP_STEPS + SIB_STEPS
    attends = kv_heads * batches
    per = max(pieces // batches, 1)
    steps = c_base + max(chunks, pieces + (attends - 1) * per)

    def one_step(t, carry):
        @pl.when(t < chunks)
        def _():
            build(t)
            remote(0, t, sib_s.at[t], sib_r.at[t], sibling).start()

        i = t - r_base

        @pl.when(valid(i))
        def _():
            remote(0, i, sib_s.at[i], sib_r.at[i], sibling).wait_recv()
            x[i] = x[i] + sib_r[i]

        gather_in(t)
        across(t)
        spread(t)
        i_c = t - c_base

        @pl.when(valid(i_c))
        def _():
            remote(5, i_c, kvf.at[core, i_c], kvf.at[1 - core, i_c], sibling).wait_recv()

        late = t - c_base - (pieces - 1)

        @pl.when(late == 0)
        def _():
            q_copy.wait()

        @pl.when((late >= 0) & (late < attends * per) & (lax.rem(late, per) == 0))
        def _():
            m = lax.div(late, per)
            attend(m)
            result_copy(m).start()

        return carry

    lax.fori_loop(0, steps, one_step, 0)

    def drain(i, carry):
        remote(0, i, sib_s.at[i], sib_r.at[i], sibling).wait_send()
        share_copy(i).wait_send()
        at = root(i)
        for used, copy in (
            (p1 < at, in_up_copy),
            (p1 > at, in_dn_copy),
            ((p1 == at) & (p2 < l2 - 1), up_copy),
            ((p1 == at) & (p2 > 0), dn_copy),
            ((p1 >= at) & (p1 < l1 - 1), out_up_copy),
            ((p1 <= at) & (p1 > 0), out_dn_copy),
        ):
            @pl.when(used)
            def _():
                copy(i).wait_send()

        return carry

    lax.fori_loop(0, chunks, drain, 0)

    def drain_result(m, carry):
        result_copy(m).wait()
        return carry

    lax.fori_loop(0, attends, drain_result, 0)


def solution(mesh):
    ring = mesh.shape["ctx"]

    def body(queries, new_keys, new_values, prefix_keys, prefix_values, pool_keys, pool_values, owners, lengths):
        heads = queries.shape[1] // HD
        kv_heads = new_keys.shape[1] // HD
        pieces = pool_keys.shape[1] * CUTS
        chunks = kv_heads * pieces
        c_rows = pool_keys.shape[2] // CUTS + prefix_keys.shape[0] * ring // pieces
        chunk_buf = pltpu.VMEM((chunks, c_rows, HD), jnp.bfloat16)
        vm = pl.BlockSpec(memory_space=pltpu.VMEM)
        hbm = pl.BlockSpec(memory_space=pl.ANY)
        sm = pl.BlockSpec(memory_space=pltpu.SMEM)
        return pl.pallas_call(
            functools.partial(kernel, ring, heads, kv_heads),
            out_shape=jax.ShapeDtypeStruct(queries.shape, jnp.bfloat16),
            in_specs=[hbm] + [vm] * 6 + [sm] * 2,
            out_specs=hbm,
            scratch_shapes=[chunk_buf] * 9
            + [
                pltpu.VMEM((2, chunks, c_rows, HD), jnp.bfloat16),
                pltpu.VMEM((queries.shape[0], queries.shape[0]), jnp.float32),
                pltpu.VMEM(queries.shape, jnp.bfloat16),
                pltpu.VMEM(queries.shape, jnp.bfloat16),
                pltpu.SemaphoreType.DMA((8, chunks)),
                pltpu.SemaphoreType.DMA((8, chunks)),
                pltpu.SemaphoreType.DMA,
                pltpu.SemaphoreType.DMA((heads // HEADS_AT_ONCE,)),
            ],
            compiler_params=pltpu.CompilerParams(
                collective_id=0, has_side_effects=True, vmem_limit_bytes=67043328
            ),
        )(queries, new_keys, new_values, prefix_keys, prefix_values, pool_keys, pool_values, owners, lengths)

    two = P(("groups", "ctx"), None)
    four = P(("groups", "ctx"), None, None, None)
    return jax.shard_map(
        body, mesh=mesh, in_specs=(two,) * 5 + (four,) * 2 + (P("groups"), P(("groups", "ctx"))),
        out_specs=two, check_vma=False,
    )
```

time: 62.9 us -> 56.3 us (0.90)
  Pallas kernels: 58.9 us -> 52.3 us
    pallas_call x1, Pallas kernels: 58.9 us -> 52.3 us  [body(): pl.pallas_call(functools.partial(kernel, ring, heads, kv_heads), out_shap...]
where the time goes in v2:
time: 56.3 us; the launch traced here: 56.1 us
  Pallas kernels  52.3 us (93%)
  local copies, waits for them, and re-layouts  3.1 us (6%)
  between operations  0.66 us (1%)
    pallas_call x1, Pallas kernels, body(): pl.pallas_call(functools.partial(kernel, ring, heads, kv_heads), out_shap...  52.3 us
    unnamed x1, local copies, waits for them, and re-layouts  3.1 us

profile of v2, /device:TPU:0, one launch (start us, length us, event | category | flops | bytes accessed | tf_op | source)
XLA Modules:
  0.0 56.1 jit_solution(10701008518514533845)
XLA Ops:
  0.7 52.3 %shard_map.91 = bf16[128,8192]{1,0:T(8,128)(2,1)} custom-call(bf16[128,8192]{1,0:T(8,128)(2,1)} %q_hbm.1, bf16[128,1024]{1,0:T(8,128)(2,1)} %nk_ref.1, bf16[128,1024]{1,0:T(8,128)(2,1)} %nv_ref.1, bf16[8,1024]{1,0:T(8,128)(2,1)} %pk_ref.1, bf16[8,1024]{1,0:T(8,128)(2,1)} %pv_ref.1, bf16[1,2,256,1024]{3,2,1,0:T(8,128)(2,1)} %poolk_ref.1, ...), custom_call_target="tpu_custom_call" | custom-call | tf_op jit(solution)/shard_map/pallas_call | solution.py:414
  53.0 3.1 %copy.12 = bf16[128,8192]{1,0:T(8,128)(2,1)} copy(bf16[128,8192]{1,0:T(8,128)(2,1)} %shard_map.91) | data formatting | bytes 4194304

commit v3 on v2

--- a/solution.py
+++ b/solution.py
@@ -12,6 +12,7 @@
 HOP_STEPS = 3
 CUTS = 1
 HEADS_AT_ONCE = 4
+SUB = 2
 
 
 def grid_of(ring):
@@ -307,25 +308,26 @@
     def attend(m):
         g, part = lax.div(m, batches), lax.rem(m, batches)
         first = g * group + part * HEADS_AT_ONCE
-        q = jnp.concatenate([q_ref[:, cols(first + j)] for j in range(HEADS_AT_ONCE)], axis=0)
         keys = kvf[0, pl.ds(g * pieces, pieces)].reshape(all_rows, HD)
         values = kvf[1, pl.ds(g * pieces, pieces)].reshape(all_rows, HD)
         dims = (((1,), (1,)), ((), ()))
-        s_far = lax.dot_general(q, keys, dims, preferred_element_type=jnp.float32)
-        s_own = lax.dot_general(q, nk_ref[:, cols(g)], dims, preferred_element_type=jnp.float32)
-        s_own = s_own + jnp.concatenate([bias[...]] * HEADS_AT_ONCE, axis=0)
-        top = jnp.maximum(jnp.max(s_far, axis=1, keepdims=True), jnp.max(s_own, axis=1, keepdims=True))
-        w_far = jnp.exp2((s_far - top) * score_scale).astype(jnp.bfloat16)
-        w_own = jnp.exp2((s_own - top) * score_scale).astype(jnp.bfloat16)
         v_far = jnp.concatenate([values, jnp.ones_like(values)], axis=1)
-        own = nv_ref[:, cols(g)]
-        v_own = jnp.concatenate([own, jnp.ones_like(own)], axis=1)
-        summed = jnp.dot(w_far, v_far, preferred_element_type=jnp.float32)
-        summed += jnp.dot(w_own, v_own, preferred_element_type=jnp.float32)
-        result = summed[:, :HD] / summed[:, HD:]
-        for j in range(HEADS_AT_ONCE):
-            piece = jnp.where(live, result[j * rows : (j + 1) * rows], 0.0)
-            out_ref[:, cols(first + j)] = piece.astype(out_ref.dtype)
+        own_k, own_v = nk_ref[:, cols(g)], nv_ref[:, cols(g)]
+        v_own = jnp.concatenate([own_v, jnp.ones_like(own_v)], axis=1)
+        mask = jnp.concatenate([bias[...]] * SUB, axis=0)
+        for sub in range(0, HEADS_AT_ONCE, SUB):
+            q = jnp.concatenate([q_ref[:, cols(first + sub + j)] for j in range(SUB)], axis=0)
+            s_far = lax.dot_general(q, keys, dims, preferred_element_type=jnp.float32)
+            s_own = lax.dot_general(q, own_k, dims, preferred_element_type=jnp.float32) + mask
+            top = jnp.maximum(jnp.max(s_far, axis=1, keepdims=True), jnp.max(s_own, axis=1, keepdims=True))
+            w_far = jnp.exp2((s_far - top) * score_scale).astype(jnp.bfloat16)
+            w_own = jnp.exp2((s_own - top) * score_scale).astype(jnp.bfloat16)
+            summed = jnp.dot(w_far, v_far, preferred_element_type=jnp.float32)
+            summed += jnp.dot(w_own, v_own, preferred_element_type=jnp.float32)
+            result = summed[:, :HD] / summed[:, HD:]
+            for j in range(SUB):
+                piece = jnp.where(live, result[j * rows : (j + 1) * rows], 0.0)
+                out_ref[:, cols(first + sub + j)] = piece.astype(out_ref.dtype)
 
     hops = max(2 * (short // 2) + long - 1, 2 * (long // 2) + short - 1)
     c_base = SIB_STEPS + hops * HOP_STEPS + SIB_STEPS

time: 56.3 us -> 55 us (0.977)
  Pallas kernels: 52.3 us -> 51 us
    pallas_call x1, Pallas kernels: 52.3 us -> 51 us  [body(): pl.pallas_call(functools.partial(kernel, ring, heads, kv_heads), out_shap...]
where the time goes in v3:
time: 55 us; the launch traced here: 54.8 us
  Pallas kernels  51 us (93%)
  local copies, waits for them, and re-layouts  3.1 us (6%)
  between operations  0.66 us (1%)
    pallas_call x1, Pallas kernels, body(): pl.pallas_call(functools.partial(kernel, ring, heads, kv_heads), out_shap...  51 us
    unnamed x1, local copies, waits for them, and re-layouts  3.1 us

profile of v3, /device:TPU:0, one launch (start us, length us, event | category | flops | bytes accessed | tf_op | source)
XLA Modules:
  0.0 54.8 jit_solution(17648590070841496743)
XLA Ops:
  0.7 51.0 %shard_map.91 = bf16[128,8192]{1,0:T(8,128)(2,1)} custom-call(bf16[128,8192]{1,0:T(8,128)(2,1)} %q_hbm.1, bf16[128,1024]{1,0:T(8,128)(2,1)} %nk_ref.1, bf16[128,1024]{1,0:T(8,128)(2,1)} %nv_ref.1, bf16[8,1024]{1,0:T(8,128)(2,1)} %pk_ref.1, bf16[8,1024]{1,0:T(8,128)(2,1)} %pv_ref.1, bf16[1,2,256,1024]{3,2,1,0:T(8,128)(2,1)} %poolk_ref.1, ...), custom_call_target="tpu_custom_call" | custom-call | tf_op jit(solution)/shard_map/pallas_call | solution.py:416
  51.7 3.1 %copy.12 = bf16[128,8192]{1,0:T(8,128)(2,1)} copy(bf16[128,8192]{1,0:T(8,128)(2,1)} %shard_map.91) | data formatting | bytes 4194304
